TPU v7x, 32 devices: a whole 2x2x4 slice. The times are simulated.
32 devices in a mesh: fsdp: 8 (over z, x), side: 4 (over y, core).
Axes of the slice: x: 2, y: 2, z: 4, core: 2. Of those that a mesh axis runs over, the one named last changes fastest.
Arguments:
- attn_inputs: bfloat16 [4096, 5120], P(('side', 'fsdp')), may hold values from -6 to 6
- queries: bfloat16 [4096, 2560], P(('side', 'fsdp')), may hold values from -310 to 310
- key_vectors: bfloat16 [4096, 512], P(('side', 'fsdp')), may hold values from -12 to 12
- logp_grad: bfloat16 [4096, 2560], P(('side', 'fsdp')), may hold values from -24 to 24
- new_logp: float32 [4096], P(('side', 'fsdp')), may hold values from -6.5 to -0.01
- old_logp: float32 [4096], P(('side', 'fsdp')), may hold values from -4 to -0.05
- rewards: float32 [8], replicated, may hold values from -8 to 8
- group_ids: int32 [8], replicated, may hold values from 0 to 1
- lengths: int32 [8], replicated, may hold values from 256 to 512
- value_proj: bfloat16 [5120, 512], P('fsdp'), may hold values from -0.078125 to 0.078125
- first_moment: bfloat16 [5120, 512], P(('fsdp', 'side')), may hold values from -120 to 120
- second_moment: bfloat16 [5120, 512], P(('fsdp', 'side')), may hold values from 100 to 9984
Outputs:
- input_grad: bfloat16 [4096, 5120], P(('side', 'fsdp'))
- new_proj: bfloat16 [5120, 512], P('fsdp')
- new_first: bfloat16 [5120, 512], P(('fsdp', 'side'))
- new_second: bfloat16 [5120, 512], P(('fsdp', 'side'))
All inputs are finite; a program needn't handle non-finite values.
Results may differ from a plain program's by a relative error of at most 0.03.
Values may be sent and summed in bfloat16 or wider, within the bound.
No kernel may reach another device: no remote copies, remote signals or barrier semaphores. Data moves between devices by JAX's collectives and lax.ppermute only.
A program may use at most 64 MiB of HBM per device.

v0:
```python
import math
import jax
import jax.numpy as jnp
from jax import lax
from jax.sharding import PartitionSpec as P

QH = 20
KVH = 4
HEAD = 128
ROLLS = 2
clip_low = 0.8
clip_high = 1.2
decay_first = 0.9
decay_second = 0.95
step_rate = 0.001
weight_decay = 0.1
adam_eps = 1e-08
bias_first = 1.0 - 0.9**10
bias_second = 1.0 - 0.95**10


def advantages(rewards, group_ids):
    group_count = rewards.shape[0] // 4
    member = (group_ids[:, None] == jnp.arange(group_count, dtype=jnp.int32)[None, :]).astype(
        jnp.float32
    )
    counts = jnp.maximum(jnp.sum(member, axis=0), 1.0)
    group_mean = jnp.sum(member * rewards[:, None], axis=0) / counts
    own_mean = jnp.sum(member * group_mean[None, :], axis=1)
    spread = rewards - own_mean
    variance = jnp.sum(member * (spread * spread)[:, None], axis=0) / counts
    own_std = jnp.sqrt(jnp.sum(member * variance[None, :], axis=1))
    return spread / jnp.maximum(own_std, 1.0)


def coefficient(new_lp, old_lp, adv_tok, len_tok, pos_tok, full_len):
    ratio_now = jnp.exp(new_lp - old_lp)
    clipped = jnp.clip(ratio_now, clip_low, clip_high)
    active = (ratio_now * adv_tok <= clipped * adv_tok) & (pos_tok < len_tok)
    len_weight = full_len / len_tok.astype(jnp.float32)
    return jnp.where(active, -adv_tok * ratio_now * len_weight, 0.0)


def block_values(query_blk, grad_blk, roll_keys, first_pos):
    tok_rows = query_blk.shape[0]
    key_count = roll_keys.shape[0]
    per_group = QH // KVH
    score_scale = 1.0 / math.sqrt(HEAD)
    query_pos = first_pos + jnp.arange(tok_rows, dtype=jnp.int32)
    key_pos = jnp.arange(key_count, dtype=jnp.int32)
    allowed = jnp.tile(key_pos[None, :] <= query_pos[:, None], (per_group, 1))
    pieces = []
    for kv_head in range(KVH):
        col_low = kv_head * per_group * HEAD
        col_high = col_low + per_group * HEAD
        q_part = (
            query_blk[:, col_low:col_high]
            .reshape(tok_rows, per_group, HEAD)
            .transpose(1, 0, 2)
            .reshape(per_group * tok_rows, HEAD)
        )
        g_part = (
            grad_blk[:, col_low:col_high]
            .reshape(tok_rows, per_group, HEAD)
            .transpose(1, 0, 2)
            .reshape(per_group * tok_rows, HEAD)
        )
        k_part = roll_keys[:, kv_head * HEAD : (kv_head + 1) * HEAD]
        scores = jnp.dot(q_part, k_part.T, preferred_element_type=jnp.float32) * score_scale
        scores = jnp.where(allowed, scores, -1e30)
        top_val = jnp.max(scores, axis=1, keepdims=True)
        expo = jnp.exp(scores - top_val)
        attention = (expo / jnp.sum(expo, axis=1, keepdims=True)).astype(jnp.bfloat16)
        pieces.append(jnp.dot(attention.T, g_part, preferred_element_type=jnp.float32))
    return jnp.concatenate(pieces, axis=1)


def adam_rows(old_rows, grad_rows, first_moment, second_moment):
    first = decay_first * first_moment.astype(jnp.float32) + (1.0 - decay_first) * grad_rows
    second = (
        decay_second * second_moment.astype(jnp.float32)
        + (1.0 - decay_second) * grad_rows * grad_rows
    )
    weight_now = old_rows.astype(jnp.float32)
    update = (
        first / bias_first / (jnp.sqrt(second / bias_second) + adam_eps) + weight_decay * weight_now
    )
    return (
        (weight_now - step_rate * update).astype(jnp.bfloat16),
        first.astype(jnp.bfloat16),
        second.astype(jnp.bfloat16),
    )


def shards(
    attn_inputs,
    queries,
    key_vectors,
    logp_grad,
    new_logp,
    old_logp,
    rewards,
    group_ids,
    lengths,
    value_proj,
    first_moment,
    second_moment,
):
    fsdp_size = lax.axis_size("fsdp")
    fsdp_index = lax.axis_index("fsdp")
    side_index = lax.axis_index("side")
    tok_rows = attn_inputs.shape[0]
    half = tok_rows // ROLLS
    full_len = half * fsdp_size
    width = key_vectors.shape[1]
    first_pos = fsdp_index * half
    advantage = advantages(rewards, group_ids)
    slot = jnp.arange(tok_rows, dtype=jnp.int32)
    global_roll = side_index * ROLLS + slot // half
    position = first_pos + slot % half
    coeff = coefficient(
        new_logp, old_logp, advantage[global_roll], lengths[global_roll], position, full_len
    )
    out_grad = (coeff[:, None] * logp_grad.astype(jnp.float32)).astype(jnp.bfloat16)
    in_columns = lax.all_to_all(attn_inputs, "fsdp", split_axis=1, concat_axis=0, tiled=True)
    all_keys = lax.all_gather(key_vectors, "fsdp", axis=0, tiled=True)
    keys_split = all_keys.reshape(fsdp_size, ROLLS, half, width)
    partials = []
    for roll in range(ROLLS):
        roll_keys = keys_split[:, roll].reshape(full_len, width)
        partials.append(
            block_values(
                queries[roll * half : (roll + 1) * half],
                out_grad[roll * half : (roll + 1) * half],
                roll_keys,
                first_pos,
            )
        )
    stacked = jnp.stack(partials, axis=0)
    placed = (
        stacked.reshape(ROLLS, fsdp_size, half, width)
        .transpose(1, 0, 2, 3)
        .reshape(fsdp_size * tok_rows, width)
    )
    values_grad = lax.psum(placed.astype(jnp.bfloat16), "fsdp")
    grad_cols = jnp.dot(values_grad, value_proj.T, preferred_element_type=jnp.float32).astype(
        jnp.bfloat16
    )
    input_grad = lax.all_to_all(grad_cols, "fsdp", split_axis=0, concat_axis=1, tiled=True)
    weight_grad = lax.dot_general(
        in_columns, values_grad, (((0,), (0,)), ((), ())), preferred_element_type=jnp.float32
    )
    shard_grad = lax.psum_scatter(
        weight_grad.astype(jnp.bfloat16), "side", scatter_dimension=0, tiled=True
    ).astype(jnp.float32)
    shard_rows = shard_grad.shape[0]
    old_rows = lax.dynamic_slice_in_dim(value_proj, side_index * shard_rows, shard_rows, 0)
    new_rows, new_first, new_second = adam_rows(old_rows, shard_grad, first_moment, second_moment)
    new_proj = lax.all_gather(new_rows, "side", axis=0, tiled=True)
    return (input_grad, new_proj, new_first, new_second)


def solution(mesh):
    placed = (
        P(("side", "fsdp"), None),
        P(("side", "fsdp"), None),
        P(("side", "fsdp"), None),
        P(("side", "fsdp"), None),
        P(("side", "fsdp")),
        P(("side", "fsdp")),
        P(),
        P(),
        P(),
        P("fsdp", None),
        P(("fsdp", "side"), None),
        P(("fsdp", "side"), None),
    )
    return jax.shard_map(
        shards,
        mesh=mesh,
        in_specs=placed,
        out_specs=(
            P(("side", "fsdp"), None),
            P("fsdp", None),
            P(("fsdp", "side"), None),
            P(("fsdp", "side"), None),
        ),
        check_vma=False,
    )
```

profile of v0, /device:TPU:0, one launch (start us, length us, event | category | flops | bytes accessed | tf_op | source)
XLA Modules:
  0.0 208.1 jit_solution(15375847009809611103)
XLA Ops:
  7.2 0.7 all-gather.2.cloned.1.call-update
  7.9 2.4 %copy.153 = bf16[128,5120]{0,1:T(8,128)(2,1)} copy(bf16[128,5120]{1,0:T(8,128)(2,1)} %param.12) | data formatting | bytes 2621440 | tf_op args[0]
  10.4 7.4 %all-to-all-start.1 = ((bf16[128,8,640]{0,2,1:T(8,128)(2,1)}), bf16[128,8,640]{0,2,1:T(8,128)(2,1)S(1)}, u32[]{:S(2)}, u32[]{:S(2)}) async-start(bf16[128,8,640]{0,2,1:T(8,128)(2,1)} %bitcast.61), calls=%async_computation.1 | async-start | bytes 2621440 | tf_op jit(solution)/shard_map/all_to_all | solution.py:125
  18.4 0.7 fusion.40
  19.1 0.7 fusion.41
  19.7 10.1 %and_select_fusion = f32[128]{0:T(128)S(1)} fusion(f32[128]{0:T(128)S(1)} %copy-done.10, f32[128]{0:T(128)S(1)} %copy-done.11, s32[]{:T(128)} %bitcast.16, f32[]{:T(128)} %bitcast.7, s32[]{:T(128)} %bitcast.17, f32[]{:T(128)} %bitcast.8, s32[]{:T(128)} %bitcast.18, f32[]{:T(128)} %bitcast.9, s32[]{:T(128)} %bitcast.19, f32[]{:T(128)} %bitcast.10, ...), kind=kLoop, calls=%fused_computation.78 | loop fusion | flops 6784 | bytes 1608 | tf_op jit(solution)/shard_map/jit(_where)/select_n | solution.py:41
  30.3 0.7 copy-done.2
  32.9 0.6 copy.149
  33.8 28.8 %all-gather.2.cloned.1.call-done = bf16[1024,512]{1,0:T(8,128)(2,1)} async-done(((bf16[128,512]{1,0:T(8,128)(2,1)}), bf16[1024,512]{1,0:T(8,128)(2,1)}) %all-gather.2.cloned.1.call-update) | async-done | bytes 1048592 | tf_op jit(solution)/shard_map/all_gather | solution.py:126
  62.7 1.3 fusion.37
  71.1 1.0 copy.141
  73.9 0.8 copy-done
  74.8 1.1 copy.151
  75.9 77.6 %all-reduce.2.cloned.1.call-done = bf16[1024,512]{1,0:T(8,128)(2,1)} async-done(((bf16[1024,512]{1,0:T(8,128)(2,1)}), bf16[1024,512]{1,0:T(8,128)(2,1)}) %all-reduce.2.cloned.1.call-update) | async-done | bytes 1048592 | tf_op jit(solution)/shard_map/psum | solution.py:145
  153.5 3.3 %convolution_convert_fusion = bf16[1024,640]{1,0:T(8,128)(2,1)} fusion(bf16[1024,512]{1,0:T(8,128)(2,1)} %all-reduce.2.cloned.1.call-done, bf16[640,512]{1,0:T(8,128)(2,1)S(1)} %copy-done.6), kind=kOutput, calls=%fused_computation | convolution fusion | flops 671744000 | bytes 3014656 | tf_op jit(solution)/shard_map/dot_general | solution.py:146
  156.8 4.2 %all-to-all-start = ((bf16[8,128,640]{2,1,0:T(8,128)(2,1)}), bf16[8,128,640]{2,1,0:T(8,128)(2,1)S(1)}, u32[]{:S(2)}, u32[]{:S(2)}) async-start(bf16[8,128,640]{2,1,0:T(8,128)(2,1)} %bitcast.127), calls=%async_computation | async-start | bytes 2621440 | tf_op jit(solution)/shard_map/all_to_all | solution.py:149
  161.0 1.5 copy.154
  162.5 2.7 %fusion = bf16[640,512]{0,1:T(8,128)(2,1)S(1)} fusion(bf16[1024,512]{1,0:T(8,128)(2,1)} %all-reduce.2.cloned.1.call-done, bf16[1024,640]{1,0:T(8,128)(2,1)} %bitcast.129), kind=kOutput, calls=%fused_computation.3 | convolution fusion | flops 671416320 | bytes 3014656 | tf_op jit(solution)/shard_map/dot_general | solution.py:150
  165.2 1.1 copy.156
  166.3 23.9 %reduce-scatter.4.cloned.1.call-done = bf16[160,512]{1,0:T(8,128)(2,1)} async-done(((bf16[640,512]{1,0:T(8,128)(2,1)}), bf16[160,512]{1,0:T(8,128)(2,1)}) %reduce-scatter.4.cloned.1.call-update) | async-done | bytes 163856 | tf_op jit(solution)/shard_map/reduce_scatter | solution.py:153
  190.2 1.9 fusion.23
  192.2 7.3 %all_gather.7 = bf16[640,512]{1,0:T(8,128)(2,1)S(1)} all-gather(bf16[160,512]{1,0:T(8,128)(2,1)S(1)} %get-tuple-element.47), channel_id=1, replica_groups=mesh['fsdp'=8,'side'=4] {'side'}, dimensions={0}, use_global_device_ids=true | all-gather | bytes 819200 | tf_op jit(solution)/shard_map/all_gather | solution.py:159
  199.5 1.2 copy.158
  200.7 0.8 copy.169
  (102 shorter events, 12.0 us)
Async XLA Ops:
  7.2 55.5 %all-gather.2.cloned.1.call-start = ((), (), s32[]{:S(2)}) async-start(), calls=%async_computation.3 | async-start | bytes 1179648 | tf_op jit(solution)/shard_map/all_gather | solution.py:126
  10.3 7.5 %copy-start.8 = (f32[8]{0:T(128)S(1)}, f32[8]{0:T(128)}, u32[]{:S(2)}) copy-start(f32[8]{0:T(128)} %param.18) | copy-start | bytes 100
  10.3 7.5 %copy-start.9 = (s32[8]{0:T(128)S(1)}, s32[8]{0:T(128)}, u32[]{:S(2)}) copy-start(s32[8]{0:T(128)} %param.19) | copy-start | bytes 100
  10.3 8.7 %copy-start.7 = (s32[8]{0:T(128)S(1)}, s32[8]{0:T(128)}, u32[]{:S(2)}) copy-start(s32[8]{0:T(128)} %param.20) | copy-start | bytes 100
  10.3 9.4 %copy-start.10 = (f32[128]{0:T(128)S(1)}, f32[128]{0:T(128)}, u32[]{:S(2)}) copy-start(f32[128]{0:T(128)} %param.16) | copy-start | bytes 1540
  10.4 9.4 %copy-start.11 = (f32[128]{0:T(128)S(1)}, f32[128]{0:T(128)}, u32[]{:S(2)}) copy-start(f32[128]{0:T(128)} %param.17) | copy-start | bytes 1540
  10.4 19.5 %copy-start.1 = (bf16[128,2560]{1,0:T(8,128)(2,1)S(1)}, bf16[128,2560]{1,0:T(8,128)(2,1)}, u32[]{:S(2)}) copy-start(bf16[128,2560]{1,0:T(8,128)(2,1)} %param.15) | copy-start | bytes 1966084
  10.4 146.4 %all-to-all-start.1 = ((bf16[128,8,640]{0,2,1:T(8,128)(2,1)}), bf16[128,8,640]{0,2,1:T(8,128)(2,1)S(1)}, u32[]{:S(2)}, u32[]{:S(2)}) async-start(bf16[128,8,640]{0,2,1:T(8,128)(2,1)} %bitcast.61), calls=%async_computation.1 | async-start | bytes 2621440 | tf_op jit(solution)/shard_map/all_to_all | solution.py:125
  17.8 135.7 %all-reduce.2.cloned.1.call-start = ((), (), s32[]{:S(2)}) async-start(), calls=%async_computation.4 | async-start | bytes 2097152 | tf_op jit(solution)/shard_map/psum | solution.py:145
  29.8 1.1 copy-start.2
  72.4 0.9 copy-start.5
  73.6 1.0 copy-start
  74.8 78.7 %copy-start.6 = (bf16[640,512]{1,0:T(8,128)(2,1)S(1)}, bf16[640,512]{1,0:T(8,128)(2,1)}, u32[]{:S(2)}) copy-start(bf16[640,512]{1,0:T(8,128)(2,1)} %param.21) | copy-start | bytes 1966084
  156.8 42.7 %all-to-all-start = ((bf16[8,128,640]{2,1,0:T(8,128)(2,1)}), bf16[8,128,640]{2,1,0:T(8,128)(2,1)S(1)}, u32[]{:S(2)}, u32[]{:S(2)}) async-start(bf16[8,128,640]{2,1,0:T(8,128)(2,1)} %bitcast.127), calls=%async_computation | async-start | bytes 2621440 | tf_op jit(solution)/shard_map/all_to_all | solution.py:149
  161.0 29.2 %reduce-scatter.4.cloned.1.call-start = ((), (), s32[]{:S(2)}) async-start(), calls=%async_computation.5 | async-start | bytes 819200 | tf_op jit(solution)/shard_map/reduce_scatter | solution.py:153
  165.2 25.1 %copy-start.3 = (bf16[160,512]{1,0:T(8,128)(2,1)S(1)}, bf16[160,512]{1,0:T(8,128)(2,1)}, u32[]{:S(2)}) copy-start(bf16[160,512]{1,0:T(8,128)(2,1)} %param.23) | copy-start | bytes 491524
  165.2 25.1 %copy-start.4 = (bf16[160,512]{1,0:T(8,128)(2,1)S(1)}, bf16[160,512]{1,0:T(8,128)(2,1)}, u32[]{:S(2)}) copy-start(bf16[160,512]{1,0:T(8,128)(2,1)} %param.22) | copy-start | bytes 491524
Sparse Core Ops, SparseCore 0:
  10.1 52.5 all-gather.1
  76.0 77.4 all-reduce.1
  166.4 23.7 reduce-scatter.3
where the time goes:
time: 209 us; the launch traced here: 208 us
  waiting for transfers between devices  131 us (63%)
  local copies, waits for them, and re-layouts  16.8 us (8%)
  other arithmetic  15.1 us (7%)
  between operations  14.2 us (7%)
  matrix products  11.8 us (6%)
  starting transfers between devices  11.7 us (6%)
  blocking collectives  7.31 us (3%)
    psum x1, waiting for transfers between devices, shards(): values_grad = lax.psum(placed.astype(jnp.bfloat16), 'fsdp')  77.6 us
    all_gather x1, waiting for transfers between devices, shards(): all_keys = lax.all_gather(key_vectors, 'fsdp', axis=0, tiled=True)  28.8 us
    reduce_scatter x1, waiting for transfers between devices, shards(): lax.psum_scatter(weight_grad.astype(jnp.bfloat16), 'side', scatter_dimens...  23.9 us
    select_n x1, other arithmetic, coefficient(): return jnp.where(active, -adv_tok * ratio_now * len_weight, 0.0)  10.1 us
    all_to_all x1, starting transfers between devices, shards(): lax.all_to_all(attn_inputs, 'fsdp', split_axis=1, concat_axis=0, tiled=True)  7.42 us
    all_gather x1, blocking collectives, shards(): new_proj = lax.all_gather(new_rows, 'side', axis=0, tiled=True)  7.31 us
    unnamed x27, local copies, waits for them, and re-layouts  6.41 us
    all_to_all x1, starting transfers between devices, shards(): lax.all_to_all(grad_cols, 'fsdp', split_axis=0, concat_axis=1, tiled=True)  4.21 us
  transfers between devices with their start and end apart: 5, of which 3 were waited for; matrix products, arithmetic and copies ran while one was open for 19% of the time, Pallas kernels for 0%

commit v1 on v0

--- a/solution.py
+++ b/solution.py
@@ -123,7 +123,12 @@
     )
     out_grad = (coeff[:, None] * logp_grad.astype(jnp.float32)).astype(jnp.bfloat16)
     in_columns = lax.all_to_all(attn_inputs, "fsdp", split_axis=1, concat_axis=0, tiled=True)
-    all_keys = lax.all_gather(key_vectors, "fsdp", axis=0, tiled=True)
+    ring = [key_vectors]
+    for hop in range(7):
+        ring.append(lax.ppermute(ring[-1], "fsdp", [(dev, (dev + 1) % 8) for dev in range(8)]))
+    all_keys = jnp.roll(
+        jnp.concatenate(ring[::-1], axis=0), (lax.axis_index("fsdp") + 1) * ring[0].shape[0], axis=0
+    )
     keys_split = all_keys.reshape(fsdp_size, ROLLS, half, width)
     partials = []
     for roll in range(ROLLS):

time: 209 us -> 233 us (1.11)
  waiting for transfers between devices: 131 us -> 143 us
  starting transfers between devices: 11.7 us -> 19.8 us
  local copies, waits for them, and re-layouts: 16.8 us -> 20.5 us
    ppermute x0 -> x7, waiting for transfers between devices: none -> 41.4 us  [shards(): lax.ppermute(ring[-1], 'fsdp', [(dev, (dev + 1) % 8) for dev in range(8)])]
    all_gather x1 -> x0, waiting for transfers between devices: 28.8 us -> none  [shards(): all_keys = lax.all_gather(key_vectors, 'fsdp', axis=0, tiled=True)]
    ppermute x0 -> x7, starting transfers between devices: none -> 10.5 us  [shards(): lax.ppermute(ring[-1], 'fsdp', [(dev, (dev + 1) % 8) for dev in range(8)])]
    transpose x8, local copies, waits for them, and re-layouts: 0.75 us -> 4.54 us  [block_values(): g_part = grad_blk[:, col_low:col_high].reshape(tok_rows, per_group, HEAD)...]
    all_to_all x1, starting transfers between devices: 7.42 us -> 5.01 us  [shards(): lax.all_to_all(attn_inputs, 'fsdp', split_axis=1, concat_axis=0, tiled=True)]
    unnamed x27 -> x58, local copies, waits for them, and re-layouts: 6.41 us -> 5.28 us
  transfers between devices with their start and end apart: 5 -> 11, of which waited for: 3 -> 6; matrix products, arithmetic and copies ran while one was open for 19% -> 19% of each run, Pallas kernels for 0% -> 0%
where the time goes in v1:
time: 233 us; the launch traced here: 232 us
  waiting for transfers between devices  143 us (61%)
  local copies, waits for them, and re-layouts  20.5 us (9%)
  starting transfers between devices  19.8 us (8%)
  other arithmetic  15.1 us (6%)
  between operations  14.6 us (6%)
  matrix products  11.8 us (5%)
  blocking collectives  7.29 us (3%)
    psum x1, waiting for transfers between devices, shards(): values_grad = lax.psum(placed.astype(jnp.bfloat16), 'fsdp')  77.5 us
    ppermute x7, waiting for transfers between devices, shards(): lax.ppermute(ring[-1], 'fsdp', [(dev, (dev + 1) % 8) for dev in range(8)])  41.4 us
    reduce_scatter x1, waiting for transfers between devices, shards(): lax.psum_scatter(weight_grad.astype(jnp.bfloat16), 'side', scatter_dimens...  23.9 us
    ppermute x7, starting transfers between devices, shards(): lax.ppermute(ring[-1], 'fsdp', [(dev, (dev + 1) % 8) for dev in range(8)])  10.5 us
    select_n x1, other arithmetic, coefficient(): return jnp.where(active, -adv_tok * ratio_now * len_weight, 0.0)  10.1 us
    all_gather x1, blocking collectives, shards(): new_proj = lax.all_gather(new_rows, 'side', axis=0, tiled=True)  7.29 us
    unnamed x58, local copies, waits for them, and re-layouts  5.28 us
    all_to_all x1, starting transfers between devices, shards(): lax.all_to_all(attn_inputs, 'fsdp', split_axis=1, concat_axis=0, tiled=True)  5.01 us
  transfers between devices with their start and end apart: 11, of which 6 were waited for; matrix products, arithmetic and copies ran while one was open for 19% of the time, Pallas kernels for 0%

profile of v1, /device:TPU:0, one launch (start us, length us, event | category | flops | bytes accessed | tf_op | source)
XLA Modules:
  0.0 232.0 jit_solution(806722511974436444)
XLA Ops:
  7.2 3.0 %collective-permute-start = (bf16[128,512]{1,0:T(8,128)(2,1)}, bf16[128,512]{1,0:T(8,128)(2,1)S(1)}, u32[]{:S(2)}, u32[]{:S(2)}) collective-permute-start(bf16[128,512]{1,0:T(8,128)(2,1)} %param.14), channel_id=1, source_target_pairs={{0,4},{4,8},{8,12},{12,16},{16,20},{20,24},{24,28},{28,0},{1,5},{5... | collective-permute-start | bytes 393224 | tf_op jit(solution)/shard_map/ppermute | solution.py:128
  10.2 2.4 %copy.153 = bf16[128,5120]{0,1:T(8,128)(2,1)} copy(bf16[128,5120]{1,0:T(8,128)(2,1)} %param.12) | data formatting | bytes 2621440 | tf_op args[0]
  12.7 5.0 %all-to-all-start.1 = ((bf16[128,8,640]{0,2,1:T(8,128)(2,1)}), bf16[128,8,640]{0,2,1:T(8,128)(2,1)S(1)}, u32[]{:S(2)}, u32[]{:S(2)}) async-start(bf16[128,8,640]{0,2,1:T(8,128)(2,1)} %bitcast.69), calls=%async_computation.1 | async-start | bytes 2621440 | tf_op jit(solution)/shard_map/all_to_all | solution.py:125
  18.3 2.0 collective-permute-start.1
  21.6 24.8 %collective-permute-done.1 = bf16[128,512]{1,0:T(8,128)(2,1)S(1)} collective-permute-done((bf16[128,512]{1,0:T(8,128)(2,1)S(1)}, bf16[128,512]{1,0:T(8,128)(2,1)S(1)}, u32[]{:S(2)}, u32[]{:S(2)}) %collective-permute-start.1) | collective-permute-done | bytes 131104 | tf_op jit(solution)/shard_map/ppermute | solution.py:128
  46.4 10.1 %and_select_fusion = f32[128]{0:T(128)S(1)} fusion(f32[128]{0:T(128)S(1)} %copy-done.18, f32[128]{0:T(128)S(1)} %copy-done.19, s32[]{:T(128)} %bitcast.17, f32[]{:T(128)} %bitcast.8, s32[]{:T(128)} %bitcast.18, f32[]{:T(128)} %bitcast.9, s32[]{:T(128)} %bitcast.19, f32[]{:T(128)} %bitcast.10, s32[]{:T(128)} %bitcast.20, f32[]{:T(128)} %bitcast.11, ...), kind=kLoop, calls=%fused_computation.102 | loop fusion | flops 6784 | bytes 1608 | tf_op jit(solution)/shard_map/jit(_where)/select_n | solution.py:41
  57.0 7.3 %collective-permute-done.3 = bf16[128,512]{1,0:T(8,128)(2,1)S(1)} collective-permute-done((bf16[128,512]{1,0:T(8,128)(2,1)S(1)}, bf16[128,512]{1,0:T(8,128)(2,1)S(1)}, u32[]{:S(2)}, u32[]{:S(2)}) %collective-permute-start.3) | collective-permute-done | bytes 131104 | tf_op jit(solution)/shard_map/ppermute | solution.py:128
  64.2 1.8 collective-permute-start.4
  66.7 5.1 %collective-permute-done.4 = bf16[128,512]{1,0:T(8,128)(2,1)S(1)} collective-permute-done((bf16[128,512]{1,0:T(8,128)(2,1)S(1)}, bf16[128,512]{1,0:T(8,128)(2,1)S(1)}, u32[]{:S(2)}, u32[]{:S(2)}) %collective-permute-start.4) | collective-permute-done | bytes 131104 | tf_op jit(solution)/shard_map/ppermute | solution.py:128
  72.8 1.0 reshape.227
  80.1 3.3 %collective-permute-start.6 = (bf16[128,512]{1,0:T(8,128)(2,1)S(1)}, bf16[128,512]{1,0:T(8,128)(2,1)S(1)}, u32[]{:S(2)}, u32[]{:S(2)}) collective-permute-start(bf16[128,512]{1,0:T(8,128)(2,1)S(1)} %collective-permute-done.5), channel_id=1, source_target_pairs={{0,4},{4,8},{8,12},{12,16},{16,20},{20,24},{24,28},{28,0},{1,5},{5... | collective-permute-start | bytes 393224 | tf_op jit(solution)/shard_map/ppermute | solution.py:128
  83.6 4.2 %collective-permute-done.6 = bf16[128,512]{1,0:T(8,128)(2,1)S(1)} collective-permute-done((bf16[128,512]{1,0:T(8,128)(2,1)S(1)}, bf16[128,512]{1,0:T(8,128)(2,1)S(1)}, u32[]{:S(2)}, u32[]{:S(2)}) %collective-permute-start.6) | collective-permute-done | bytes 131104 | tf_op jit(solution)/shard_map/ppermute | solution.py:128
  95.5 1.0 copy.141
  98.5 1.1 copy.151
  99.6 77.5 %all-reduce.2.cloned.1.call-done = bf16[1024,512]{1,0:T(8,128)(2,1)} async-done(((bf16[1024,512]{1,0:T(8,128)(2,1)}), bf16[1024,512]{1,0:T(8,128)(2,1)}) %all-reduce.2.cloned.1.call-update) | async-done | bytes 1048592 | tf_op jit(solution)/shard_map/psum | solution.py:150
  177.1 3.3 %convolution_convert_fusion = bf16[1024,640]{1,0:T(8,128)(2,1)} fusion(bf16[1024,512]{1,0:T(8,128)(2,1)} %all-reduce.2.cloned.1.call-done, bf16[640,512]{1,0:T(8,128)(2,1)S(1)} %copy-done.14), kind=kOutput, calls=%fused_computation | convolution fusion | flops 671744000 | bytes 3014656 | tf_op jit(solution)/shard_map/dot_general | solution.py:151
  180.4 4.2 %all-to-all-start = ((bf16[8,128,640]{2,1,0:T(8,128)(2,1)}), bf16[8,128,640]{2,1,0:T(8,128)(2,1)S(1)}, u32[]{:S(2)}, u32[]{:S(2)}) async-start(bf16[8,128,640]{2,1,0:T(8,128)(2,1)} %bitcast.160), calls=%async_computation | async-start | bytes 2621440 | tf_op jit(solution)/shard_map/all_to_all | solution.py:154
  184.6 1.5 copy.154
  186.1 2.7 %fusion = bf16[640,512]{0,1:T(8,128)(2,1)S(1)} fusion(bf16[1024,512]{1,0:T(8,128)(2,1)} %all-reduce.2.cloned.1.call-done, bf16[1024,640]{1,0:T(8,128)(2,1)} %bitcast.162), kind=kOutput, calls=%fused_computation.3 | convolution fusion | flops 671416320 | bytes 3014656 | tf_op jit(solution)/shard_map/dot_general | solution.py:155
  188.8 1.1 copy.156
  189.9 23.9 %reduce-scatter.4.cloned.1.call-done = bf16[160,512]{1,0:T(8,128)(2,1)} async-done(((bf16[640,512]{1,0:T(8,128)(2,1)}), bf16[160,512]{1,0:T(8,128)(2,1)}) %reduce-scatter.4.cloned.1.call-update) | async-done | bytes 163856 | tf_op jit(solution)/shard_map/reduce_scatter | solution.py:158
  213.9 1.9 fusion.31
  215.8 7.3 %all_gather.3 = bf16[640,512]{1,0:T(8,128)(2,1)S(1)} all-gather(bf16[160,512]{1,0:T(8,128)(2,1)S(1)} %get-tuple-element.47), channel_id=1, replica_groups=mesh['fsdp'=8,'side'=4] {'side'}, dimensions={0}, use_global_device_ids=true | all-gather | bytes 819200 | tf_op jit(solution)/shard_map/all_gather | solution.py:164
  223.1 1.2 copy.158
  (146 shorter events, 20.5 us)
Async XLA Ops:
  7.2 10.6 %copy-start.16 = (f32[8]{0:T(128)S(1)}, f32[8]{0:T(128)}, u32[]{:S(2)}) copy-start(f32[8]{0:T(128)} %param.18) | copy-start | bytes 100
  7.2 10.6 %copy-start.17 = (s32[8]{0:T(128)S(1)}, s32[8]{0:T(128)}, u32[]{:S(2)}) copy-start(s32[8]{0:T(128)} %param.19) | copy-start | bytes 100
  7.2 13.8 %copy-start.15 = (s32[8]{0:T(128)S(1)}, s32[8]{0:T(128)}, u32[]{:S(2)}) copy-start(s32[8]{0:T(128)} %param.20) | copy-start | bytes 100
  7.2 39.2 %copy-start.18 = (f32[128]{0:T(128)S(1)}, f32[128]{0:T(128)}, u32[]{:S(2)}) copy-start(f32[128]{0:T(128)} %param.16) | copy-start | bytes 1540
  7.2 39.2 %copy-start.19 = (f32[128]{0:T(128)S(1)}, f32[128]{0:T(128)}, u32[]{:S(2)}) copy-start(f32[128]{0:T(128)} %param.17) | copy-start | bytes 1540
  7.2 49.6 %copy-start.1 = (bf16[128,2560]{1,0:T(8,128)(2,1)S(1)}, bf16[128,2560]{1,0:T(8,128)(2,1)}, u32[]{:S(2)}) copy-start(bf16[128,2560]{1,0:T(8,128)(2,1)} %param.15) | copy-start | bytes 1966084
  7.2 11.0 %collective-permute-start = (bf16[128,512]{1,0:T(8,128)(2,1)}, bf16[128,512]{1,0:T(8,128)(2,1)S(1)}, u32[]{:S(2)}, u32[]{:S(2)}) collective-permute-start(bf16[128,512]{1,0:T(8,128)(2,1)} %param.14), channel_id=1, source_target_pairs={{0,4},{4,8},{8,12},{12,16},{16,20},{20,24},{24,28},{28,0},{1,5},{5... | collective-permute-start | bytes 393224 | tf_op jit(solution)/shard_map/ppermute | solution.py:128
  12.7 53.4 %copy-start.2 = (bf16[128,2560]{1,0:T(8,128)(2,1)S(1)}, bf16[128,2560]{1,0:T(8,128)(2,1)}, u32[]{:S(2)}) copy-start(bf16[128,2560]{1,0:T(8,128)(2,1)} %param.13) | copy-start | bytes 1966084
  12.7 167.7 %all-to-all-start.1 = ((bf16[128,8,640]{0,2,1:T(8,128)(2,1)}), bf16[128,8,640]{0,2,1:T(8,128)(2,1)S(1)}, u32[]{:S(2)}, u32[]{:S(2)}) async-start(bf16[128,8,640]{0,2,1:T(8,128)(2,1)} %bitcast.69), calls=%async_computation.1 | async-start | bytes 2621440 | tf_op jit(solution)/shard_map/all_to_all | solution.py:125
  17.7 159.4 %all-reduce.2.cloned.1.call-start = ((), (), s32[]{:S(2)}) async-start(), calls=%async_computation.3 | async-start | bytes 2097152 | tf_op jit(solution)/shard_map/psum | solution.py:150
  18.3 28.1 %collective-permute-start.1 = (bf16[128,512]{1,0:T(8,128)(2,1)S(1)}, bf16[128,512]{1,0:T(8,128)(2,1)S(1)}, u32[]{:S(2)}, u32[]{:S(2)}) collective-permute-start(bf16[128,512]{1,0:T(8,128)(2,1)S(1)} %collective-permute-done), channel_id=1, source_target_pairs={{0,4},{4,8},{8,12},{12,16},{16,20},{20,24},{24,28},{28,0},{1,5},{5... | collective-permute-start | bytes 393224 | tf_op jit(solution)/shard_map/ppermute | solution.py:128
  46.4 10.1 %collective-permute-start.2 = (bf16[128,512]{1,0:T(8,128)(2,1)S(1)}, bf16[128,512]{1,0:T(8,128)(2,1)S(1)}, u32[]{:S(2)}, u32[]{:S(2)}) collective-permute-start(bf16[128,512]{1,0:T(8,128)(2,1)S(1)} %collective-permute-done.1), channel_id=1, source_target_pairs={{0,4},{4,8},{8,12},{12,16},{16,20},{20,24},{24,28},{28,0},{1,5},{5... | collective-permute-start | bytes 393224 | tf_op jit(solution)/shard_map/ppermute | solution.py:128
  56.5 7.7 %collective-permute-start.3 = (bf16[128,512]{1,0:T(8,128)(2,1)S(1)}, bf16[128,512]{1,0:T(8,128)(2,1)S(1)}, u32[]{:S(2)}, u32[]{:S(2)}) collective-permute-start(bf16[128,512]{1,0:T(8,128)(2,1)S(1)} %collective-permute-done.2), channel_id=1, source_target_pairs={{0,4},{4,8},{8,12},{12,16},{16,20},{20,24},{24,28},{28,0},{1,5},{5... | collective-permute-start | bytes 393224 | tf_op jit(solution)/shard_map/ppermute | solution.py:128
  64.2 7.7 %collective-permute-start.4 = (bf16[128,512]{1,0:T(8,128)(2,1)S(1)}, bf16[128,512]{1,0:T(8,128)(2,1)S(1)}, u32[]{:S(2)}, u32[]{:S(2)}) collective-permute-start(bf16[128,512]{1,0:T(8,128)(2,1)S(1)} %collective-permute-done.3), channel_id=1, source_target_pairs={{0,4},{4,8},{8,12},{12,16},{16,20},{20,24},{24,28},{28,0},{1,5},{5... | collective-permute-start | bytes 393224 | tf_op jit(solution)/shard_map/ppermute | solution.py:128
  66.7 7.7 %copy-start.4 = (bf16[64,640]{1,0:T(8,128)(2,1)S(1)}, bf16[64,640]{1,0:T(8,128)(2,1)}, u32[]{:S(2)}) copy-start(bf16[64,640]{1,0:T(8,128)(2,1)} %get-tuple-element.35) | copy-start | bytes 245764
  71.9 8.2 %collective-permute-start.5 = (bf16[128,512]{1,0:T(8,128)(2,1)S(1)}, bf16[128,512]{1,0:T(8,128)(2,1)S(1)}, u32[]{:S(2)}, u32[]{:S(2)}) collective-permute-start(bf16[128,512]{1,0:T(8,128)(2,1)S(1)} %collective-permute-done.4), channel_id=1, source_target_pairs={{0,4},{4,8},{8,12},{12,16},{16,20},{20,24},{24,28},{28,0},{1,5},{5... | collective-permute-start | bytes 393224 | tf_op jit(solution)/shard_map/ppermute | solution.py:128
  78.1 9.8 %copy-start.3 = (bf16[128,512]{1,0:T(8,128)(2,1)S(1)}, bf16[128,512]{1,0:T(8,128)(2,1)}, u32[]{:S(2)}) copy-start(bf16[128,512]{1,0:T(8,128)(2,1)} %param.14) | copy-start | bytes 393220
  80.1 7.7 %collective-permute-start.6 = (bf16[128,512]{1,0:T(8,128)(2,1)S(1)}, bf16[128,512]{1,0:T(8,128)(2,1)S(1)}, u32[]{:S(2)}, u32[]{:S(2)}) collective-permute-start(bf16[128,512]{1,0:T(8,128)(2,1)S(1)} %collective-permute-done.5), channel_id=1, source_target_pairs={{0,4},{4,8},{8,12},{12,16},{16,20},{20,24},{24,28},{28,0},{1,5},{5... | collective-permute-start | bytes 393224 | tf_op jit(solution)/shard_map/ppermute | solution.py:128
  90.1 1.4 copy-start.7
  98.5 78.6 %copy-start.14 = (bf16[640,512]{1,0:T(8,128)(2,1)S(1)}, bf16[640,512]{1,0:T(8,128)(2,1)}, u32[]{:S(2)}) copy-start(bf16[640,512]{1,0:T(8,128)(2,1)} %param.21) | copy-start | bytes 1966084
  180.4 42.7 %all-to-all-start = ((bf16[8,128,640]{2,1,0:T(8,128)(2,1)}), bf16[8,128,640]{2,1,0:T(8,128)(2,1)S(1)}, u32[]{:S(2)}, u32[]{:S(2)}) async-start(bf16[8,128,640]{2,1,0:T(8,128)(2,1)} %bitcast.160), calls=%async_computation | async-start | bytes 2621440 | tf_op jit(solution)/shard_map/all_to_all | solution.py:154
  184.6 29.3 %reduce-scatter.4.cloned.1.call-start = ((), (), s32[]{:S(2)}) async-start(), calls=%async_computation.4 | async-start | bytes 819200 | tf_op jit(solution)/shard_map/reduce_scatter | solution.py:158
  186.1 27.8 %copy-start.5 = (bf16[160,512]{1,0:T(8,128)(2,1)S(1)}, bf16[160,512]{1,0:T(8,128)(2,1)}, u32[]{:S(2)}) copy-start(bf16[160,512]{1,0:T(8,128)(2,1)} %param.23) | copy-start | bytes 491524
  186.1 27.8 %copy-start.6 = (bf16[160,512]{1,0:T(8,128)(2,1)S(1)}, bf16[160,512]{1,0:T(8,128)(2,1)}, u32[]{:S(2)}) copy-start(bf16[160,512]{1,0:T(8,128)(2,1)} %param.22) | copy-start | bytes 491524
  (7 other events, 6.6 us)
Sparse Core Ops, SparseCore 0:
  99.7 77.3 all-reduce.1
  190.0 23.7 reduce-scatter.3
